TPU v7x, 256 devices: a whole 4x4x8 slice. The times are simulated.
256 devices in a mesh: dom: 64 (over z, x, core), rep: 4 (over y).
Axes of the slice: x: 4, y: 4, z: 8, core: 2. Of those that a mesh axis runs over, the one named last changes fastest.
Arguments:
- entities: bfloat16 [65536, 512], P('dom'), may hold values from -60 to 60
- relations: bfloat16 [4, 512, 512], replicated, may hold values from -2 to 2
- head_local: int32 [131072], P(('dom', 'rep')), may hold values from 0 to 1023
- rel_ids: int32 [131072], P(('dom', 'rep')), may hold values from 0 to 3
- tail_part: int32 [131072, 1], P(('dom', 'rep')), may hold values from 0 to 63; in each aligned block of 512 rows (0 to 511, 512 to 1023, ...) at most 16 rows name the same one
- tail_local: int32 [131072], P(('dom', 'rep')), may hold values from 0 to 1023
- neg_local: int32 [2048], P('dom'), may hold values from 0 to 1023
Outputs:
- entity_grad: float32 [65536, 512], P('dom')
- relation_grad: float32 [4, 512, 512], replicated
- edge_loss: float32 [131072], P(('dom', 'rep'))
Inputs may be any that keep to these rules, and one draw needn't show every extreme that they name: `tail_part`: in the 512 edges of one device no partition is named by more than 16 edges, a bound that some block reaches.
All inputs are finite; a program needn't handle non-finite values.
Results may differ from a plain program's by a relative error of at most 0.012.
The roundings to bfloat16 on the way count: a program that leaves them out, or rounds other values in their place, can miss the bound.
Values may be sent and summed in bfloat16 or wider, within the bound.
A program may use at most 64 MiB of HBM per device.

v0:
```python
import math
import jax
import jax.numpy as jnp
from jax import lax
from jax.sharding import PartitionSpec as P

D = 512


def local(entities, relations, head_local, rel_ids, tail_part, tail_local, neg_local):
    factor = 1.0 / math.sqrt(D)
    ent_dev = entities.shape[0]
    columns = entities.shape[1]
    edge_count = head_local.shape[0]
    part_count = lax.axis_size("dom")
    capacity = 2 * edge_count // part_count
    slot_count = part_count * capacity
    relation_count = relations.shape[0]
    head_rows = jnp.take(entities, head_local, axis=0)
    selectors = [(rel_ids == relation)[:, None] for relation in range(relation_count)]
    query_sum = jnp.zeros((edge_count, columns), jnp.float32)
    for relation in range(relation_count):
        picked = jnp.where(selectors[relation], head_rows, jnp.zeros_like(head_rows))
        query_sum = query_sum + jnp.dot(
            picked, relations[relation], preferred_element_type=jnp.float32
        )
    queries = query_sum.astype(jnp.bfloat16)
    target = tail_part[:, 0]
    target_hot = (target[:, None] == jnp.arange(part_count, dtype=jnp.int32)[None, :]).astype(
        jnp.int32
    )
    earlier = jnp.cumsum(target_hot, axis=0) - target_hot
    position = jnp.sum(earlier * target_hot, axis=1)
    slot_index = target * capacity + position
    slot_match = (slot_index[None, :] == jnp.arange(slot_count, dtype=jnp.int32)[:, None]).astype(
        jnp.int32
    )
    filled = jnp.sum(slot_match, axis=1) > 0
    source = jnp.sum(slot_match * jnp.arange(edge_count, dtype=jnp.int32)[None, :], axis=1)
    send_ids = jnp.where(filled, jnp.take(tail_local, source, axis=0), 0).reshape(
        part_count, capacity
    )
    recv_ids = lax.all_to_all(send_ids, "dom", split_axis=0, concat_axis=0, tiled=True)
    looked_up = jnp.take(entities, recv_ids.reshape(-1), axis=0).reshape(
        part_count, capacity, columns
    )
    returned = lax.all_to_all(looked_up, "dom", split_axis=0, concat_axis=0, tiled=True)
    tail_embed = jnp.take(returned.reshape(slot_count, columns), slot_index, axis=0)
    own_negs = jnp.take(entities, neg_local, axis=0)
    negatives = lax.all_gather(own_negs, "dom", axis=0, tiled=True)
    positive = (
        jnp.sum(queries.astype(jnp.float32) * tail_embed.astype(jnp.float32), axis=1) * factor
    )
    scores = (
        lax.dot_general(
            queries, negatives, (((1,), (1,)), ((), ())), preferred_element_type=jnp.float32
        )
        * factor
    )
    row_max = jnp.maximum(positive, jnp.max(scores, axis=1))
    exp_pos = jnp.exp(positive - row_max)
    exp_neg = jnp.exp(scores - row_max[:, None])
    partition_sum = exp_pos + jnp.sum(exp_neg, axis=1)
    edge_loss = jnp.log(partition_sum) + row_max - positive
    prob_pos = exp_pos / partition_sum
    prob_neg = (exp_neg / partition_sum[:, None]).astype(jnp.bfloat16)
    mixed = jnp.dot(prob_neg, negatives, preferred_element_type=jnp.float32)
    query_grad = (
        factor * ((prob_pos - 1.0)[:, None] * tail_embed.astype(jnp.float32) + mixed)
    ).astype(jnp.bfloat16)
    tail_grad = factor * (prob_pos - 1.0)[:, None] * queries.astype(jnp.float32)
    neg_grad = factor * lax.dot_general(
        prob_neg, queries, (((0,), (0,)), ((), ())), preferred_element_type=jnp.float32
    )
    head_grad = jnp.zeros((edge_count, columns), jnp.float32)
    rel_terms = []
    for relation in range(relation_count):
        picked_grad = jnp.where(selectors[relation], query_grad, jnp.zeros_like(query_grad))
        head_grad = head_grad + lax.dot_general(
            picked_grad,
            relations[relation],
            (((1,), (1,)), ((), ())),
            preferred_element_type=jnp.float32,
        )
        picked_rows = jnp.where(selectors[relation], head_rows, jnp.zeros_like(head_rows))
        rel_terms.append(
            lax.dot_general(
                picked_rows,
                query_grad,
                (((0,), (0,)), ((), ())),
                preferred_element_type=jnp.float32,
            )
        )
    relation_grad = lax.psum(jnp.stack(rel_terms), ("dom", "rep"))
    grad_send = jnp.where(filled[:, None], jnp.take(tail_grad, source, axis=0), 0.0)
    grad_recv = lax.all_to_all(
        grad_send.reshape(part_count, capacity, columns),
        "dom",
        split_axis=0,
        concat_axis=0,
        tiled=True,
    )
    owned = lax.psum_scatter(neg_grad, "dom", scatter_dimension=0, tiled=True)
    target_ids = jnp.concatenate([head_local, recv_ids.reshape(-1), neg_local])
    target_rows = jnp.concatenate(
        [head_grad, grad_recv.reshape(slot_count, columns), owned], axis=0
    )
    block_rows = min(512, ent_dev)
    block_count = ent_dev // block_rows

    def add_block(start):
        hot = (
            target_ids[None, :] == (start + jnp.arange(block_rows, dtype=jnp.int32))[:, None]
        ).astype(jnp.float32)
        return jnp.dot(
            hot, target_rows, precision=lax.Precision.HIGHEST, preferred_element_type=jnp.float32
        )

    local_grad = lax.map(add_block, jnp.arange(block_count, dtype=jnp.int32) * block_rows).reshape(
        ent_dev, columns
    )
    entity_grad = lax.psum(local_grad, "rep")
    return (entity_grad, relation_grad, edge_loss)


def solution(mesh):
    return jax.shard_map(
        local,
        mesh=mesh,
        in_specs=(
            P("dom", None),
            P(),
            P(("dom", "rep")),
            P(("dom", "rep")),
            P(("dom", "rep"), None),
            P(("dom", "rep")),
            P("dom"),
        ),
        out_specs=(P("dom", None), P(), P(("dom", "rep"))),
        check_vma=False,
    )
```

profile of v0, /device:TPU:1, one launch (start us, length us, event | category | flops | bytes accessed | tf_op | source)
XLA Modules:
  0.0 596.3 jit_solution(15604910715601647900)
XLA Ops:
  7.2 0.7 compare_select_fusion.7
  8.0 0.7 compare_and_fusion.4
  8.7 0.6 gather_fusion.2
  9.3 0.7 broadcast_select_fusion.23
  10.0 0.7 fusion.56
  10.7 1.2 reduce-window.6
  12.2 0.8 fusion.55
  13.0 0.7 compare_and_fusion.2
  13.7 0.7 select_reduce_fusion
  14.5 6.9 %gather_fusion = s32[1024]{0:T(1024)S(1)} fusion(s32[512]{0:T(512)S(1)} %copy-done.1, s32[1024]{0:T(1024)S(1)} %broadcast_clamp_fusion.1), kind=kCustom, calls=%fused_computation.2 | custom fusion | bytes 12288 | tf_op jit(solution)/shard_map/jit(_take)/gather | solution.py:40
  21.5 22.2 %all_to_all.16 = s32[64,1,16]{2,1,0:T(1,128)S(1)} all-to-all(s32[64,1,16]{2,1,0:T(1,128)S(1)} %bitcast.90), channel_id=1, replica_groups=mesh['dom'=64,'rep'=4] {'dom'}, dimensions={0} | all-to-all | bytes 8192 | tf_op jit(solution)/shard_map/all_to_all | solution.py:43
  43.8 4.0 gather_fusion.1
  47.8 1.2 broadcast_select_fusion
  49.0 4.8 all-to-all-start.1
  54.0 2.0 gather_fusion.4
  56.3 1.7 fusion.23
  58.7 1.5 convolution_add_fusion.4
  60.1 24.6 %all-to-all-done.1 = bf16[64,16,512]{2,1,0:T(8,128)(2,1)S(1)} async-done(((bf16[64,16,512]{2,1,0:T(8,128)(2,1)}), bf16[64,16,512]{2,1,0:T(8,128)(2,1)S(1)}, u32[]{:S(2)}, u32[]{:S(2)}) %all-to-all-start.1) | async-done | bytes 1048608 | tf_op jit(solution)/shard_map/all_to_all | solution.py:47
  84.7 2.0 gather_fusion.5
  86.9 2.1 fusion.14
  89.0 5.9 all-gather.2.cloned.1.call-done
  94.9 3.0 multiply_reduce_fusion
  97.9 0.8 fusion.10
  98.7 0.6 broadcast_multiply_fusion
  99.3 0.8 divide_convert_fusion
  100.2 1.3 copy-done.2
  101.5 3.3 convolution_multiply_fusion
  105.5 4.9 gather_fusion.3
  110.3 2.7 select_select_fusion
  113.1 6.7 %all-to-all-start.2 = ((f32[64,16,512]{2,1,0:T(8,128)}), f32[64,16,512]{2,1,0:T(8,128)}, u32[]{:S(2)}, u32[]{:S(2)}) async-start(f32[64,16,512]{2,1,0:T(8,128)} %select_select_fusion), calls=%async_computation.2 | async-start | bytes 4194304 | tf_op jit(solution)/shard_map/all_to_all | solution.py:96
  120.6 0.7 reduce.7
  121.4 3.1 fusion.12
  126.4 2.4 pad_maximum_fusion
  128.9 1.0 copy-done.7
  129.9 1.7 fusion.21
  133.2 36.2 %all-to-all-done.2 = f32[64,16,512]{2,1,0:T(8,128)} async-done(((f32[64,16,512]{2,1,0:T(8,128)}), f32[64,16,512]{2,1,0:T(8,128)}, u32[]{:S(2)}, u32[]{:S(2)}) %all-to-all-start.2) | async-done | bytes 2097184 | tf_op jit(solution)/shard_map/all_to_all | solution.py:96
  169.4 71.1 %reduce-scatter.2.cloned.1.call-done = f32[32,512]{1,0:T(8,128)} async-done(((f32[2048,512]{1,0:T(8,128)}), f32[32,512]{1,0:T(8,128)}) %reduce-scatter.2.cloned.1.call-update) | async-done | bytes 65552 | tf_op jit(solution)/shard_map/reduce_scatter | solution.py:103
  240.4 3.6 pad_maximum_fusion.1
  244.1 14.5 %while.10 = (s32[]{:T(128)}, f32[2,512,512]{2,1,0:T(8,128)}, s32[1568]{0:T(1024)S(1)}, s32[2]{0:T(128)S(1)}, f32[1568,512]{1,0:T(8,128)}, /*index=5*/s32[]{:T(128)}) while((s32[]{:T(128)}, f32[2,512,512]{2,1,0:T(8,128)}, s32[1568]{0:T(1024)S(1)}, s32[2]{0:T(128)S(1)}, f32[1568,512]{1,0:T(8,128)}, /*index=5*/s32[]{:T(128)}) %tuple.34), condition=%wide.region_10.12_spmd, body=%wide.region_9.11_spmd.sunk | while | flops 4933304832 | bytes 4270305 | solution.py:119
  244.1 0.6 dynamic_slice.5
  244.6 0.6 iota_add_fusion.2
  245.2 6.1 %fusion.94 = f32[2,512,512]{2,1,0:T(8,128)} fusion(f32[2,512,512]{2,1,0:T(8,128)} %get-tuple-element.97, s32[]{:T(128)S(6)} %copy.37, f32[1568,512]{1,0:T(8,128)} %get-tuple-element.106, s32[1568]{0:T(1024)S(1)} %get-tuple-element.104, s32[512]{0:T(512)S(1)} %iota_add_fusion.2), kind=kOutput, calls=%fused_computation.11.clone.1 | convolution fusion | flops 4933304320 | bytes 4268164 | tf_op jit(solution)/shard_map/while/body/eval_jaxpr/dot_general | solution.py:115
  251.9 0.6 iota_add_fusion.2
  252.5 6.1 %fusion.94 = f32[2,512,512]{2,1,0:T(8,128)} fusion(f32[2,512,512]{2,1,0:T(8,128)} %get-tuple-element.97, s32[]{:T(128)S(6)} %copy.37, f32[1568,512]{1,0:T(8,128)} %get-tuple-element.106, s32[1568]{0:T(1024)S(1)} %get-tuple-element.104, s32[512]{0:T(512)S(1)} %iota_add_fusion.2), kind=kOutput, calls=%fused_computation.11.clone.1 | convolution fusion | flops 4933304320 | bytes 4268164 | tf_op jit(solution)/shard_map/while/body/eval_jaxpr/dot_general | solution.py:115
  258.6 258.9 %all-reduce.5.cloned.1.call-done = f32[4,512,512]{2,1,0:T(8,128)} async-done(((f32[4,512,512]{2,1,0:T(8,128)}), f32[4,512,512]{2,1,0:T(8,128)}) %all-reduce.5.cloned.1.call-update) | async-done | bytes 4194320 | tf_op jit(solution)/shard_map/psum | solution.py:94
  517.5 67.0 %all-reduce.3.cloned.1.call-done = f32[1024,512]{1,0:T(8,128)} async-done(((f32[1024,512]{1,0:T(8,128)}), f32[1024,512]{1,0:T(8,128)}) %all-reduce.3.cloned.1.call-update) | async-done | bytes 2097168 | tf_op jit(solution)/shard_map/psum | solution.py:122
  584.5 3.2 copy.45
  587.7 2.0 copy.46
  (78 shorter events, 7.7 us)
Async XLA Ops:
  7.2 1.5 copy-start
  7.2 7.4 %copy-start.1 = (s32[512]{0:T(512)S(1)}, s32[512]{0:T(512)}, u32[]{:S(2)}) copy-start(s32[512]{0:T(512)} %param.16) | copy-start | bytes 6148
  7.2 87.7 %all-gather.2.cloned.1.call-start = ((), (), s32[]{:S(2)}) async-start(), calls=%async_computation.4 | async-start | bytes 2129920 | tf_op jit(solution)/shard_map/all_gather | solution.py:50
  47.8 6.2 %copy-start.12 = (s32[512]{0:T(512)S(1)}, s32[512]{0:T(512)}, u32[]{:S(2)}) copy-start(s32[512]{0:T(512)} %param.13) | copy-start | bytes 6148
  49.0 35.7 %all-to-all-start.1 = ((bf16[64,16,512]{2,1,0:T(8,128)(2,1)}), bf16[64,16,512]{2,1,0:T(8,128)(2,1)S(1)}, u32[]{:S(2)}, u32[]{:S(2)}) async-start(bf16[64,16,512]{2,1,0:T(8,128)(2,1)} %broadcast_select_fusion), calls=%async_computation.1 | async-start | bytes 2097152 | tf_op jit(solution)/shard_map/all_to_all | solution.py:47
  53.8 186.7 %reduce-scatter.2.cloned.1.call-start = ((), (), s32[]{:S(2)}) async-start(), calls=%async_computation.5 | async-start | bytes 4259840 | tf_op jit(solution)/shard_map/reduce_scatter | solution.py:103
  54.0 2.3 copy-start.13
  56.2 30.7 %copy-start.4 = (bf16[512,512]{0,1:T(8,128)(2,1)}, bf16[512,512]{0,1:T(8,128)(2,1)S(1)}, u32[]{:S(2)}) copy-start(bf16[512,512]{0,1:T(8,128)(2,1)S(1)} %copy.27) | copy-start | bytes 1572868
  56.2 1.9 copy-start.9
  86.9 2.1 copy-start.11
  100.2 1.3 copy-start.2
  113.1 8.3 %copy-start.14 = (s32[32]{0:T(128)S(1)}, s32[32]{0:T(128)}, u32[]{:S(2)}) copy-start(s32[32]{0:T(128)} %param.17) | copy-start | bytes 388
  113.1 8.3 %copy-start.3 = (bf16[512,2048]{1,0:T(8,128)(2,1)S(1)}, bf16[512,2048]{1,0:T(8,128)(2,1)}, u32[]{:S(2)}) copy-start(bf16[512,2048]{1,0:T(8,128)(2,1)} %copy-done.2) | copy-start | bytes 6291460
  113.1 56.3 %all-to-all-start.2 = ((f32[64,16,512]{2,1,0:T(8,128)}), f32[64,16,512]{2,1,0:T(8,128)}, u32[]{:S(2)}, u32[]{:S(2)}) async-start(f32[64,16,512]{2,1,0:T(8,128)} %select_select_fusion), calls=%async_computation.2 | async-start | bytes 4194304 | tf_op jit(solution)/shard_map/all_to_all | solution.py:96
  119.8 397.7 %all-reduce.5.cloned.1.call-start = ((), (), s32[]{:S(2)}) async-start(), calls=%async_computation.7 | async-start | bytes 8388608 | tf_op jit(solution)/shard_map/psum | solution.py:94
  121.4 3.1 copy-start.5
  124.5 1.4 copy-start.6
  128.8 1.1 copy-start.7
  128.9 455.6 %all-reduce.3.cloned.1.call-start = ((), (), s32[]{:S(2)}) async-start(), calls=%async_computation.6 | async-start | bytes 4194304 | tf_op jit(solution)/shard_map/psum | solution.py:122
  129.9 1.8 copy-start.10
  584.5 3.2 copy-start.8
Sparse Core Ops, SparseCore 0:
  10.8 84.0 all-gather.1
  104.9 135.4 reduce-scatter.1
  246.8 270.6 all-reduce.4
  520.3 64.1 all-reduce.2
where the time goes:
time: 597 us; the launch traced here: 596 us
  waiting for transfers between devices  464 us (78%)
  matrix products  32.5 us (5%)
  local copies, waits for them, and re-layouts  31.2 us (5%)
  blocking collectives  22.2 us (4%)
  other arithmetic  20.5 us (3%)
  between operations  14.2 us (2%)
  starting transfers between devices  12 us (2%)
    psum x1, waiting for transfers between devices, local(): relation_grad = lax.psum(jnp.stack(rel_terms), ('dom', 'rep'))  259 us
    reduce_scatter x1, waiting for transfers between devices, local(): owned = lax.psum_scatter(neg_grad, 'dom', scatter_dimension=0, tiled=True)  71.1 us
    psum x1, waiting for transfers between devices, local(): entity_grad = lax.psum(local_grad, 'rep')  67 us
    all_to_all x1, waiting for transfers between devices, local(): lax.all_to_all(grad_send.reshape(part_count, capacity, columns), 'dom', s...  36.2 us
    all_to_all x1, waiting for transfers between devices, local(): lax.all_to_all(looked_up, 'dom', split_axis=0, concat_axis=0, tiled=True)  24.6 us
    all_to_all x1, blocking collectives, local(): lax.all_to_all(send_ids, 'dom', split_axis=0, concat_axis=0, tiled=True)  22.2 us
    dot_general x2, matrix products, add_block(): jnp.dot(hot, target_rows, precision=lax.Precision.HIGHEST, preferred_elem...  12.3 us
  transfers between devices with their start and end apart: 6, of which 6 were waited for; matrix products, arithmetic and copies ran while one was open for 11% of the time, Pallas kernels for 0%

commit v1 on v0

--- a/solution.py
+++ b/solution.py
@@ -119,7 +119,8 @@
     local_grad = lax.map(add_block, jnp.arange(block_count, dtype=jnp.int32) * block_rows).reshape(
         ent_dev, columns
     )
-    entity_grad = lax.psum(local_grad, "rep")
+    pieces = lax.all_gather(local_grad, "rep", axis=0, tiled=False)
+    entity_grad = pieces.sum(axis=0)
     return (entity_grad, relation_grad, edge_loss)
 
 

time: 597 us -> 635 us (1.064)
  waiting for transfers between devices: 464 us -> 497 us
  other arithmetic: 20.5 us -> 27.7 us
    all_gather x0 -> x1, waiting for transfers between devices: none -> 83.8 us  [local(): pieces = lax.all_gather(local_grad, 'rep', axis=0, tiled=False)]
    psum x1 -> x0, waiting for transfers between devices: 67 us -> none  [local(): entity_grad = lax.psum(local_grad, 'rep')]
    psum x1, waiting for transfers between devices: 259 us -> 269 us  [local(): relation_grad = lax.psum(jnp.stack(rel_terms), ('dom', 'rep'))]
    all_to_all x1, waiting for transfers between devices: 36.2 us -> 42.8 us  [local(): lax.all_to_all(grad_send.reshape(part_count, capacity, columns), 'dom', s...]
  transfers between devices with their start and end apart: 6 -> 6, of which waited for: 6 -> 6; matrix products, arithmetic and copies ran while one was open for 11% -> 8% of each run, Pallas kernels for 0% -> 0%
where the time goes in v1:
time: 635 us; the launch traced here: 634 us
  waiting for transfers between devices  497 us (78%)
  local copies, waits for them, and re-layouts  30.6 us (5%)
  matrix products  30 us (5%)
  other arithmetic  27.7 us (4%)
  blocking collectives  22.2 us (3%)
  between operations  14.2 us (2%)
  starting transfers between devices  12.2 us (2%)
    psum x1, waiting for transfers between devices, local(): relation_grad = lax.psum(jnp.stack(rel_terms), ('dom', 'rep'))  269 us
    all_gather x1, waiting for transfers between devices, local(): pieces = lax.all_gather(local_grad, 'rep', axis=0, tiled=False)  83.8 us
    reduce_scatter x1, waiting for transfers between devices, local(): owned = lax.psum_scatter(neg_grad, 'dom', scatter_dimension=0, tiled=True)  69.1 us
    all_to_all x1, waiting for transfers between devices, local(): lax.all_to_all(grad_send.reshape(part_count, capacity, columns), 'dom', s...  42.8 us
    all_to_all x1, waiting for transfers between devices, local(): lax.all_to_all(looked_up, 'dom', split_axis=0, concat_axis=0, tiled=True)  25.9 us
    all_to_all x1, blocking collectives, local(): lax.all_to_all(send_ids, 'dom', split_axis=0, concat_axis=0, tiled=True)  22.2 us
  transfers between devices with their start and end apart: 6, of which 6 were waited for; matrix products, arithmetic and copies ran while one was open for 8% of the time, Pallas kernels for 0%

profile of v1, /device:TPU:1, one launch (start us, length us, event | category | flops | bytes accessed | tf_op | source)
XLA Modules:
  0.0 633.6 jit_solution(1067248375319757793)
XLA Ops:
  7.2 0.7 compare_select_fusion.7
  8.0 0.7 compare_and_fusion.4
  8.7 0.6 gather_fusion.2
  9.3 0.7 broadcast_select_fusion.23
  10.0 0.7 fusion.56
  10.7 1.2 reduce-window.6
  12.2 0.8 fusion.55
  13.0 0.7 compare_and_fusion.2
  13.7 0.7 select_reduce_fusion
  14.6 6.9 %gather_fusion = s32[1024]{0:T(1024)S(1)} fusion(s32[512]{0:T(512)S(1)} %copy-done.2, s32[1024]{0:T(1024)S(1)} %broadcast_clamp_fusion.1), kind=kCustom, calls=%fused_computation.2 | custom fusion | bytes 12288 | tf_op jit(solution)/shard_map/jit(_take)/gather | solution.py:40
  21.5 22.2 %all_to_all.16 = s32[64,1,16]{2,1,0:T(1,128)S(1)} all-to-all(s32[64,1,16]{2,1,0:T(1,128)S(1)} %bitcast.90), channel_id=1, replica_groups=mesh['dom'=64,'rep'=4] {'dom'}, dimensions={0} | all-to-all | bytes 8192 | tf_op jit(solution)/shard_map/all_to_all | solution.py:43
  43.8 4.0 gather_fusion.1
  47.8 1.2 broadcast_select_fusion
  49.0 4.8 all-to-all-start.1
  54.0 2.0 gather_fusion.4
  56.3 1.7 fusion.23
  59.2 25.9 %all-to-all-done.1 = bf16[64,16,512]{2,1,0:T(8,128)(2,1)S(1)} async-done(((bf16[64,16,512]{2,1,0:T(8,128)(2,1)}), bf16[64,16,512]{2,1,0:T(8,128)(2,1)S(1)}, u32[]{:S(2)}, u32[]{:S(2)}) %all-to-all-start.1) | async-done | bytes 1048608 | tf_op jit(solution)/shard_map/all_to_all | solution.py:47
  85.0 2.0 gather_fusion.5
  87.2 1.8 fusion.14
  89.0 6.3 all-gather.3.cloned.1.call-done
  95.3 3.0 multiply_reduce_fusion
  98.3 0.8 fusion.10
  99.1 0.6 broadcast_multiply_fusion
  99.7 0.8 divide_convert_fusion
  100.6 3.3 convolution_multiply_fusion
  104.1 1.1 convert_multiply_fusion.2
  105.2 1.6 copy.30
  106.8 4.9 gather_fusion.3
  111.7 2.8 select_select_fusion
  114.5 6.9 %all-to-all-start.2 = ((f32[64,16,512]{2,1,0:T(8,128)}), f32[64,16,512]{2,1,0:T(8,128)}, u32[]{:S(2)}, u32[]{:S(2)}) async-start(f32[64,16,512]{2,1,0:T(8,128)} %select_select_fusion), calls=%async_computation.2 | async-start | bytes 4194304 | tf_op jit(solution)/shard_map/all_to_all | solution.py:96
  122.1 0.7 reduce.7
  123.0 3.1 fusion.12
  128.1 42.8 %all-to-all-done.2 = f32[64,16,512]{2,1,0:T(8,128)} async-done(((f32[64,16,512]{2,1,0:T(8,128)}), f32[64,16,512]{2,1,0:T(8,128)}, u32[]{:S(2)}, u32[]{:S(2)}) %all-to-all-start.2) | async-done | bytes 2097184 | tf_op jit(solution)/shard_map/all_to_all | solution.py:96
  170.9 69.1 %reduce-scatter.2.cloned.1.call-done = f32[32,512]{1,0:T(8,128)} async-done(((f32[2048,512]{1,0:T(8,128)}), f32[32,512]{1,0:T(8,128)}) %reduce-scatter.2.cloned.1.call-update) | async-done | bytes 65552 | tf_op jit(solution)/shard_map/reduce_scatter | solution.py:103
  240.0 3.6 pad_maximum_fusion.1
  243.6 14.7 %while.10 = (s32[]{:T(128)}, f32[2,512,512]{2,1,0:T(8,128)}, s32[1568]{0:T(1024)S(1)}, s32[2]{0:T(128)S(1)}, f32[1568,512]{1,0:T(8,128)}, /*index=5*/s32[]{:T(128)}) while((s32[]{:T(128)}, f32[2,512,512]{2,1,0:T(8,128)}, s32[1568]{0:T(1024)S(1)}, s32[2]{0:T(128)S(1)}, f32[1568,512]{1,0:T(8,128)}, /*index=5*/s32[]{:T(128)}) %tuple.34), condition=%wide.region_10.12_spmd, body=%wide.region_9.11_spmd.sunk | while | flops 4933304832 | bytes 4270305 | solution.py:119
  243.6 0.6 dynamic_slice.5
  244.2 0.6 iota_add_fusion.2
  244.8 6.1 fusion.94
  251.0 0.6 dynamic_slice.5
  251.5 0.6 iota_add_fusion.2
  252.2 6.1 fusion.94
  258.4 1.0 copy-done.4
  261.2 2.5 pad_maximum_fusion
  263.7 83.8 %all-gather.5.cloned.1.call-done = f32[4,1024,512]{2,1,0:T(8,128)} async-done(((f32[1,1024,512]{2,1,0:T(8,128)}), f32[4,1024,512]{2,1,0:T(8,128)}) %all-gather.5.cloned.1.call-update) | async-done | bytes 8388624 | tf_op jit(solution)/shard_map/all_gather | solution.py:122
  347.6 6.0 reduce_sum.68
  353.5 268.9 %all-reduce.2.cloned.1.call-done = f32[4,512,512]{2,1,0:T(8,128)} async-done(((f32[4,512,512]{2,1,0:T(8,128)}), f32[4,512,512]{2,1,0:T(8,128)}) %all-reduce.2.cloned.1.call-update) | async-done | bytes 4194320 | tf_op jit(solution)/shard_map/psum | solution.py:94
  622.4 4.7 copy.44
  (72 shorter events, 7.5 us)
Async XLA Ops:
  7.2 1.5 copy-start
  7.2 7.4 %copy-start.2 = (s32[512]{0:T(512)S(1)}, s32[512]{0:T(512)}, u32[]{:S(2)}) copy-start(s32[512]{0:T(512)} %param.16) | copy-start | bytes 6148
  7.2 88.1 %all-gather.3.cloned.1.call-start = ((), (), s32[]{:S(2)}) async-start(), calls=%async_computation.4 | async-start | bytes 2129920 | tf_op jit(solution)/shard_map/all_gather | solution.py:50
  47.8 6.2 copy-start.9
  49.0 36.0 %all-to-all-start.1 = ((bf16[64,16,512]{2,1,0:T(8,128)(2,1)}), bf16[64,16,512]{2,1,0:T(8,128)(2,1)S(1)}, u32[]{:S(2)}, u32[]{:S(2)}) async-start(bf16[64,16,512]{2,1,0:T(8,128)(2,1)} %broadcast_select_fusion), calls=%async_computation.1 | async-start | bytes 2097152 | tf_op jit(solution)/shard_map/all_to_all | solution.py:47
  53.8 186.2 %reduce-scatter.2.cloned.1.call-start = ((), (), s32[]{:S(2)}) async-start(), calls=%async_computation.5 | async-start | bytes 4259840 | tf_op jit(solution)/shard_map/reduce_scatter | solution.py:103
  54.0 2.3 copy-start.10
  56.2 31.0 %copy-start.3 = (bf16[512,512]{0,1:T(8,128)(2,1)}, bf16[512,512]{0,1:T(8,128)(2,1)S(1)}, u32[]{:S(2)}) copy-start(bf16[512,512]{0,1:T(8,128)(2,1)S(1)} %copy.27) | copy-start | bytes 1572868
  56.2 1.9 copy-start.5
  87.2 1.8 copy-start.7
  114.5 8.5 %copy-start.11 = (s32[32]{0:T(128)S(1)}, s32[32]{0:T(128)}, u32[]{:S(2)}) copy-start(s32[32]{0:T(128)} %param.17) | copy-start | bytes 388
  114.5 8.5 %copy-start.8 = (bf16[512,512]{0,1:T(8,128)(2,1)S(1)}, bf16[512,512]{0,1:T(8,128)(2,1)}, u32[]{:S(2)}) copy-start(bf16[512,512]{0,1:T(8,128)(2,1)} %copy-done.7) | copy-start | bytes 1572868
  114.5 56.5 %all-to-all-start.2 = ((f32[64,16,512]{2,1,0:T(8,128)}), f32[64,16,512]{2,1,0:T(8,128)}, u32[]{:S(2)}, u32[]{:S(2)}) async-start(f32[64,16,512]{2,1,0:T(8,128)} %select_select_fusion), calls=%async_computation.2 | async-start | bytes 4194304 | tf_op jit(solution)/shard_map/all_to_all | solution.py:96
  121.3 226.2 %all-gather.5.cloned.1.call-start = ((), (), s32[]{:S(2)}) async-start(), calls=%async_computation.6 | async-start | bytes 10485760 | tf_op jit(solution)/shard_map/all_gather | solution.py:122
  123.0 3.1 copy-start.6
  258.3 1.0 copy-start.4
  258.3 364.0 %all-reduce.2.cloned.1.call-start = ((), (), s32[]{:S(2)}) async-start(), calls=%async_computation.7 | async-start | bytes 8388608 | tf_op jit(solution)/shard_map/psum | solution.py:94
  622.4 4.7 copy-start.1
Sparse Core Ops, SparseCore 0:
  11.4 83.9 all-gather.2
  104.1 135.8 reduce-scatter.1
  258.4 89.0 all-gather.4
  354.4 267.9 all-reduce.1
